TPU v7x, 32 devices: a whole 2x2x4 slice. The times are simulated.
32 devices in a mesh: row: 16 (over z, y, x), col: 2 (over core).
Axes of the slice: x: 2, y: 2, z: 4, core: 2. Of those that a mesh axis runs over, the one named last changes fastest.
Arguments:
- features: bfloat16 [8192, 128], P(('row', 'col')), may hold values from -6 to 6
- weight: bfloat16 [128, 256], replicated, may hold values from -0.5 to 0.5
- bias: float32 [256], replicated, may hold values from -3 to 3
- grad_out: bfloat16 [8192, 256], P(('row', 'col')), may hold values from -6 to 6
- tiles: bfloat16 [32, 128, 128, 128], P(('row', 'col')), may hold values from -0.25 to 0.25
- tile_count: int32 [32], P(('row', 'col')), may hold values from 1 to 128, as said below
- tile_dst: int32 [32, 128], P(('row', 'col')), may hold values from 0 to 3
- tile_src: int32 [32, 128], P(('row', 'col')), may hold values from 0 to 9
Outputs:
- activations: bfloat16 [8192, 256], P(('row', 'col'))
- grad_features: bfloat16 [8192, 128], P(('row', 'col'))
- grad_weight: float32 [128, 256], replicated
- grad_bias: float32 [256], replicated
Inputs may be any that keep to these rules, and one draw needn't show every extreme that they name: Slots from tile_count on are ignored; some device holds 128 live slots.
All inputs are finite; a program needn't handle non-finite values.
Results may differ from a plain program's by a relative error of at most 0.019.
Values may be sent and summed in bfloat16 or wider, within the bound.
A program may use at most 64 MiB of HBM per device.

v0:
```python
import math

import jax
import jax.numpy as jnp
from jax import lax
from jax.sharding import PartitionSpec as P


def shifted(value, axis, steps):
    count = lax.axis_size(axis)
    pairs = [(source, (source + steps) % count) for source in range(count)]
    return lax.ppermute(value, axis, pairs)


def local(features, weight, bias, grad_out, tiles, tile_count, tile_dst, tile_src):
    node_dev = features.shape[0]
    in_width = features.shape[1]
    tile = tiles.shape[2]
    maxt = tiles.shape[1]
    band = 2
    tiles_dev = node_dev // tile
    n_col = lax.axis_size("col")
    dst_tiles = n_col * tiles_dev
    window_tiles = (2 * band + 1) * tiles_dev
    nodes_all = node_dev * lax.axis_size("row") * n_col
    group = math.gcd(16, maxt)
    pieces = {0: features}
    for offset in (-2, -1, 1, 2):
        pieces[offset] = shifted(features, "row", -offset)
    window = jnp.concatenate([pieces[o] for o in range(-band, band + 1)], 0).reshape(
        window_tiles, tile, in_width
    )
    tile_local = tiles[0]
    count = tile_count[0]
    dst_local = tile_dst[0]
    src_local = tile_src[0]
    turns = (count + group - 1) // group
    offsets_in = jnp.arange(group, dtype=jnp.int32)

    def forward_step(index, acc):
        start = index * group
        tile_block = lax.dynamic_slice_in_dim(tile_local, start, group, 0)
        src_block = lax.dynamic_slice_in_dim(src_local, start, group, 0)
        dst_block = lax.dynamic_slice_in_dim(dst_local, start, group, 0)
        live = (start + offsets_in < count).astype(jnp.float32)
        prod = jnp.einsum(
            "kij,kjh->kih", tile_block, window[src_block], preferred_element_type=jnp.float32
        )
        return acc.at[dst_block].add(prod * live[:, None, None])

    acc = lax.fori_loop(0, turns, forward_step, jnp.zeros((dst_tiles, tile, in_width), jnp.float32))
    summed = lax.psum_scatter(
        acc.reshape(dst_tiles * tile, in_width).astype(jnp.bfloat16),
        "col",
        scatter_dimension=0,
        tiled=True,
    )
    pre = jnp.dot(summed, weight, preferred_element_type=jnp.float32) + bias
    sig = jax.nn.sigmoid(pre)
    activations = (pre * sig).astype(jnp.bfloat16)
    dpre = (grad_out.astype(jnp.float32) * sig * (1.0 + pre * (1.0 - sig))).astype(jnp.bfloat16)
    grad_agg = lax.dot_general(
        dpre, weight, (((1,), (1,)), ((), ())), preferred_element_type=jnp.float32
    ).astype(jnp.bfloat16)
    block_grads = lax.all_gather(grad_agg, "col", axis=0, tiled=True).reshape(
        dst_tiles, tile, in_width
    )

    def back_step(index, acc_back):
        start = index * group
        tile_block = lax.dynamic_slice_in_dim(tile_local, start, group, 0)
        src_block = lax.dynamic_slice_in_dim(src_local, start, group, 0)
        dst_block = lax.dynamic_slice_in_dim(dst_local, start, group, 0)
        live = (start + offsets_in < count).astype(jnp.float32)
        contrib = jnp.einsum(
            "kji,kjh->kih", tile_block, block_grads[dst_block], preferred_element_type=jnp.float32
        )
        return acc_back.at[src_block].add(contrib * live[:, None, None])

    backs = lax.fori_loop(
        0, turns, back_step, jnp.zeros((window_tiles, tile, in_width), jnp.float32)
    )
    backs = backs.reshape(2 * band + 1, node_dev, in_width)
    total = backs[band]
    for offset in (-2, -1, 1, 2):
        total = total + shifted(backs[offset + band], "row", offset)
    grad_features = total.astype(jnp.bfloat16)
    weight_term = lax.dot_general(
        summed, dpre, (((0,), (0,)), ((), ())), preferred_element_type=jnp.float32
    )
    bias_term = jnp.sum(dpre.astype(jnp.float32), 0)
    weight_total, bias_total = lax.psum((weight_term, bias_term), ("row", "col"))
    scale = math.sqrt(nodes_all)
    grad_weight = weight_total / scale
    grad_bias = bias_total / scale
    return (activations, grad_features, grad_weight, grad_bias)


def solution(mesh):
    in_specs = (
        P(("row", "col"), None),
        P(),
        P(),
        P(("row", "col"), None),
        P(("row", "col"), None, None, None),
        P(("row", "col")),
        P(("row", "col"), None),
        P(("row", "col"), None),
    )
    out_specs = (P(("row", "col"), None), P(("row", "col"), None), P(), P())
    return jax.shard_map(local, mesh=mesh, in_specs=in_specs, out_specs=out_specs, check_vma=False)
```

profile of v0, /device:TPU:0, one launch (start us, length us, event | category | flops | bytes accessed | tf_op | source)
XLA Modules:
  0.0 247.2 jit_solution(1033797611451873253)
XLA Ops:
  7.2 3.0 %collective-permute-start = (bf16[256,128]{1,0:T(8,128)(2,1)}, bf16[256,128]{1,0:T(8,128)(2,1)S(1)}, u32[]{:S(2)}, u32[]{:S(2)}) collective-permute-start(bf16[256,128]{1,0:T(8,128)(2,1)} %param.12), channel_id=1, source_target_pairs={{0,4},{2,6},{4,8},{6,10},{8,12},{10,14},{12,16},{14,18},{16,20},{1... | collective-permute-start | bytes 196616 | tf_op jit(solution)/shard_map/ppermute | solution.py:12
  10.3 4.1 %collective-permute-start.2 = (bf16[256,128]{1,0:T(8,128)(2,1)}, bf16[256,128]{1,0:T(8,128)(2,1)S(1)}, u32[]{:S(2)}, u32[]{:S(2)}) collective-permute-start(bf16[256,128]{1,0:T(8,128)(2,1)} %param.12), channel_id=1, source_target_pairs={{0,30},{2,0},{4,2},{6,4},{8,6},{10,8},{12,10},{14,12},{16,14},{18,... | collective-permute-start | bytes 196616 | tf_op jit(solution)/shard_map/ppermute | solution.py:12
  14.4 1.9 collective-permute-start.3
  17.0 5.5 %collective-permute-done.1 = bf16[256,128]{1,0:T(8,128)(2,1)S(1)} collective-permute-done((bf16[256,128]{1,0:T(8,128)(2,1)}, bf16[256,128]{1,0:T(8,128)(2,1)S(1)}, u32[]{:S(2)}, u32[]{:S(2)}) %collective-permute-start.1) | collective-permute-done | bytes 65568 | tf_op jit(solution)/shard_map/ppermute | solution.py:12
  22.5 0.9 constant_dynamic-update-slice_fusion.2
  23.4 15.2 %while.22 = (s32[]{:T(128)}, f32[4,128,128]{2,1,0:T(8,128)S(1)}, s32[]{:T(128)}, s32[128]{0:T(128)}, bf16[128,128,128]{2,1,0:T(8,128)(2,1)}, /*index=5*/s32[128]...) while((s32[]{:T(128)}, f32[4,128,128]{2,1,0:T(8,128)S(1)}, ...), condition=%wide.region_2.3_spmd.clone, body=%wide.region_0.2_spmd.clone.sunk | while | flops 67634328 | bytes 6296307 | solution.py:51
  23.5 0.7 compare_convert_fusion.4
  24.1 0.8 compare_select_fusion.6
  24.9 0.6 gather_fusion
  25.5 1.3 convolution_multiply_fusion.4
  26.9 1.6 scatter_fusion
  28.5 0.7 compare_convert_fusion.4
  29.2 0.8 compare_select_fusion.6
  29.9 0.6 gather_fusion
  30.6 1.3 convolution_multiply_fusion.4
  31.9 1.6 scatter_fusion
  33.6 0.7 compare_convert_fusion.4
  34.2 0.8 compare_select_fusion.6
  35.0 0.6 gather_fusion
  35.6 1.3 convolution_multiply_fusion.4
  37.0 1.6 scatter_fusion
  38.6 0.7 convert_element_type.38
  39.4 6.4 %copy.12 = bf16[1,128,128,128]{2,3,1,0:T(8,128)(2,1)} copy(bf16[1,128,128,128]{3,2,1,0:T(8,128)(2,1)} %bitcast.38) | data formatting | bytes 8388608 | tf_op args[4]
  45.8 23.7 %reduce-scatter.2.cloned.1.call-done = bf16[256,128]{1,0:T(8,128)(2,1)} async-done(((bf16[512,128]{1,0:T(8,128)(2,1)}), bf16[256,128]{1,0:T(8,128)(2,1)}) %reduce-scatter.2.cloned.1.call-update) | async-done | bytes 65552 | tf_op jit(solution)/shard_map/reduce_scatter | solution.py:52
  69.6 1.8 convert_reduce_fusion
  71.3 40.4 %psum.15 = f32[256]{0:T(256)S(1)} all-reduce(f32[256]{0:T(256)S(1)} %get-tuple-element.180), channel_id=1, replica_groups=mesh['row'=16,'col'=2] {'row','col'}, use_global_device_ids=true, to_apply=%region_9.10 | all-reduce | flops 256 | bytes 2048 | tf_op jit(solution)/shard_map/psum | solution.py:92
  111.7 0.2 convolution_convert_fusion
  111.9 1.7 fusion.13
  113.6 1.9 all_gather.3
  115.6 13.1 %while.23 = (s32[]{:T(128)}, f32[10,128,128]{2,1,0:T(8,128)S(1)}, s32[]{:T(128)}, s32[128]{0:T(128)S(1)}, bf16[128,128,128]{1,2,0:T(8,128)(2,1)}, /*index=5*/s32...) while((s32[]{:T(128)}, f32[10,128,128]{2,1,0:T(8,128)S(1)}, ...), condition=%wide.region_6.7_spmd.clone, body=%wide.region_4.6_spmd.clone.sunk | while | flops 67634328 | bytes 6296307 | solution.py:80
  115.6 0.7 compare_convert_fusion.5
  116.3 0.6 gather_fusion.1
  117.0 1.3 convolution_multiply_fusion.5
  118.3 1.6 scatter_fusion.1
  120.0 0.7 compare_convert_fusion.5
  120.7 0.6 gather_fusion.1
  121.4 1.3 convolution_multiply_fusion.5
  122.7 1.6 scatter_fusion.1
  124.4 0.7 compare_convert_fusion.5
  125.1 0.6 gather_fusion.1
  125.8 1.3 convolution_multiply_fusion.5
  127.1 1.6 scatter_fusion.1
  128.8 0.6 broadcast_multiply_fusion.1
  129.3 6.7 %collective-permute-start.6 = (f32[256,128]{1,0:T(8,128)S(1)}, f32[256,128]{1,0:T(8,128)S(1)}, u32[]{:S(2)}, u32[]{:S(2)}) collective-permute-start(f32[256,128]{1,0:T(8,128)S(1)} %bitcast.44), channel_id=1, source_target_pairs={{0,2},{2,4},{4,6},{6,8},{8,10},{10,12},{12,14},{14,16},{16,18},{18... | collective-permute-start | bytes 393224 | tf_op jit(solution)/shard_map/ppermute | solution.py:12
  136.0 22.1 %collective-permute-start.4 = (f32[256,128]{1,0:T(8,128)S(1)}, f32[256,128]{1,0:T(8,128)S(1)}, u32[]{:S(2)}, u32[]{:S(2)}) collective-permute-start(f32[256,128]{1,0:T(8,128)S(1)} %bitcast.42), channel_id=1, source_target_pairs={{0,28},{2,30},{4,0},{6,2},{8,4},{10,6},{12,8},{14,10},{16,12},{18,... | collective-permute-start | bytes 393224 | tf_op jit(solution)/shard_map/ppermute | solution.py:12
  158.1 80.0 %all-reduce.2.cloned.1.call-done = f32[128,256]{1,0:T(8,128)} async-done(((f32[128,256]{1,0:T(8,128)}), f32[128,256]{1,0:T(8,128)}) %all-reduce.2.cloned.1.call-update) | async-done | bytes 131088 | tf_op jit(solution)/shard_map/psum | solution.py:92
  238.1 1.6 broadcast_multiply_fusion
  239.7 0.7 fusion.11
  (40 shorter events, 0.6 us)
Async XLA Ops:
  7.2 62.4 %copy-start = (bf16[128,256]{1,0:T(8,128)(2,1)S(1)}, bf16[128,256]{1,0:T(8,128)(2,1)}, u32[]{:S(2)}) copy-start(bf16[128,256]{1,0:T(8,128)(2,1)} %param.13) | copy-start | bytes 196612
  7.2 62.4 %reduce-scatter.2.cloned.1.call-start = ((), (), s32[]{:S(2)}) async-start(), calls=%async_computation.1 | async-start | bytes 196608 | tf_op jit(solution)/shard_map/reduce_scatter | solution.py:52
  7.2 9.7 %collective-permute-start = (bf16[256,128]{1,0:T(8,128)(2,1)}, bf16[256,128]{1,0:T(8,128)(2,1)S(1)}, u32[]{:S(2)}, u32[]{:S(2)}) collective-permute-start(bf16[256,128]{1,0:T(8,128)(2,1)} %param.12), channel_id=1, source_target_pairs={{0,4},{2,6},{4,8},{6,10},{8,12},{10,14},{12,16},{14,18},{16,20},{1... | collective-permute-start | bytes 196616 | tf_op jit(solution)/shard_map/ppermute | solution.py:12
  10.3 13.1 %collective-permute-start.2 = (bf16[256,128]{1,0:T(8,128)(2,1)}, bf16[256,128]{1,0:T(8,128)(2,1)S(1)}, u32[]{:S(2)}, u32[]{:S(2)}) collective-permute-start(bf16[256,128]{1,0:T(8,128)(2,1)} %param.12), channel_id=1, source_target_pairs={{0,30},{2,0},{4,2},{6,4},{8,6},{10,8},{12,10},{14,12},{16,14},{18,... | collective-permute-start | bytes 196616 | tf_op jit(solution)/shard_map/ppermute | solution.py:12
  14.4 8.1 %collective-permute-start.1 = (bf16[256,128]{1,0:T(8,128)(2,1)}, bf16[256,128]{1,0:T(8,128)(2,1)S(1)}, u32[]{:S(2)}, u32[]{:S(2)}) collective-permute-start(bf16[256,128]{1,0:T(8,128)(2,1)} %param.12), channel_id=1, source_target_pairs={{0,2},{2,4},{4,6},{6,8},{8,10},{10,12},{12,14},{14,16},{16,18},{18... | collective-permute-start | bytes 196616 | tf_op jit(solution)/shard_map/ppermute | solution.py:12
  14.4 9.0 %collective-permute-start.3 = (bf16[256,128]{1,0:T(8,128)(2,1)}, bf16[256,128]{1,0:T(8,128)(2,1)S(1)}, u32[]{:S(2)}, u32[]{:S(2)}) collective-permute-start(bf16[256,128]{1,0:T(8,128)(2,1)} %param.12), channel_id=1, source_target_pairs={{0,28},{2,30},{4,0},{6,2},{8,4},{10,6},{12,8},{14,10},{16,12},{18,... | collective-permute-start | bytes 196616 | tf_op jit(solution)/shard_map/ppermute | solution.py:12
  39.3 198.8 %all-reduce.2.cloned.1.call-start = ((), (), s32[]{:S(2)}) async-start(), calls=%async_computation.2 | async-start | bytes 262144 | tf_op jit(solution)/shard_map/psum | solution.py:92
  39.3 30.2 %copy-start.3 = (bf16[256,256]{1,0:T(8,128)(2,1)S(1)}, bf16[256,256]{1,0:T(8,128)(2,1)}, u32[]{:S(2)}) copy-start(bf16[256,256]{1,0:T(8,128)(2,1)} %param.15) | copy-start | bytes 393220
  39.4 30.2 %copy-start.4 = (f32[256]{0:T(256)S(1)}, f32[256]{0:T(256)}, u32[]{:S(2)}) copy-start(f32[256]{0:T(256)} %param.14) | copy-start | bytes 3076
  39.4 76.2 %copy-start.1 = (s32[128]{0:T(128)S(1)}, s32[128]{0:T(128)}, u32[]{:S(2)}) copy-start(s32[128]{0:T(128)} %get-tuple-element.397) | copy-start | bytes 1540
  39.4 76.2 %copy-start.2 = (s32[128]{0:T(128)S(1)}, s32[128]{0:T(128)}, u32[]{:S(2)}) copy-start(s32[128]{0:T(128)} %get-tuple-element.398) | copy-start | bytes 1540
  129.3 110.4 %collective-permute-start.6 = (f32[256,128]{1,0:T(8,128)S(1)}, f32[256,128]{1,0:T(8,128)S(1)}, u32[]{:S(2)}, u32[]{:S(2)}) collective-permute-start(f32[256,128]{1,0:T(8,128)S(1)} %bitcast.44), channel_id=1, source_target_pairs={{0,2},{2,4},{4,6},{6,8},{8,10},{10,12},{12,14},{14,16},{16,18},{18... | collective-permute-start | bytes 393224 | tf_op jit(solution)/shard_map/ppermute | solution.py:12
  136.0 103.7 %collective-permute-start.5 = (f32[256,128]{1,0:T(8,128)S(1)}, f32[256,128]{1,0:T(8,128)S(1)}, u32[]{:S(2)}, u32[]{:S(2)}) collective-permute-start(f32[256,128]{1,0:T(8,128)S(1)} %bitcast.43), channel_id=1, source_target_pairs={{0,30},{2,0},{4,2},{6,4},{8,6},{10,8},{12,10},{14,12},{16,14},{18,... | collective-permute-start | bytes 393224 | tf_op jit(solution)/shard_map/ppermute | solution.py:12
  136.0 103.7 %collective-permute-start.4 = (f32[256,128]{1,0:T(8,128)S(1)}, f32[256,128]{1,0:T(8,128)S(1)}, u32[]{:S(2)}, u32[]{:S(2)}) collective-permute-start(f32[256,128]{1,0:T(8,128)S(1)} %bitcast.42), channel_id=1, source_target_pairs={{0,28},{2,30},{4,0},{6,2},{8,4},{10,6},{12,8},{14,10},{16,12},{18,... | collective-permute-start | bytes 393224 | tf_op jit(solution)/shard_map/ppermute | solution.py:12
  158.1 81.6 %collective-permute-start.7 = (f32[256,128]{1,0:T(8,128)S(1)}, f32[256,128]{1,0:T(8,128)S(1)}, u32[]{:S(2)}, u32[]{:S(2)}) collective-permute-start(f32[256,128]{1,0:T(8,128)S(1)} %bitcast.41), channel_id=1, source_target_pairs={{0,4},{2,6},{4,8},{6,10},{8,12},{10,14},{12,16},{14,18},{16,20},{1... | collective-permute-start | bytes 393224 | tf_op jit(solution)/shard_map/ppermute | solution.py:12
Sparse Core Ops, SparseCore 0:
  39.4 30.0 reduce-scatter.1
  113.7 124.3 all-reduce.1
where the time goes:
time: 248 us; the launch traced here: 247 us
  waiting for transfers between devices  109 us (44%)
  blocking collectives  42.3 us (17%)
  starting transfers between devices  37.9 us (15%)
  other arithmetic  19.5 us (8%)
  between operations  14.9 us (6%)
  matrix products  11.7 us (5%)
  local copies, waits for them, and re-layouts  11.3 us (5%)
    psum x1, waiting for transfers between devices, local(): lax.psum((weight_term, bias_term), ('row', 'col'))  80 us
    psum x1, blocking collectives, local(): lax.psum((weight_term, bias_term), ('row', 'col'))  40.4 us
    ppermute x8, starting transfers between devices, shifted(): return lax.ppermute(value, axis, pairs)  37.8 us
    reduce_scatter x1, waiting for transfers between devices, local(): lax.psum_scatter(acc.reshape(dst_tiles * tile, in_width).astype(jnp.bfloa...  23.7 us
    unnamed x15, local copies, waits for them, and re-layouts  7.34 us
    ppermute x8, waiting for transfers between devices, shifted(): return lax.ppermute(value, axis, pairs)  5.53 us
  transfers between devices with their start and end apart: 10, of which 3 were waited for; matrix products, arithmetic and copies ran while one was open for 9% of the time, Pallas kernels for 0%

commit v1 on v0

v1 whole, which is shorter than its diff:
```python
import functools
import math

import jax
import jax.numpy as jnp
from jax import lax
from jax.experimental import pallas as pl
from jax.experimental.pallas import tpu as pltpu
from jax.sharding import PartitionSpec as P

MESH = pl.DeviceIdType.MESH
BAND = 2
OFFSETS = tuple(o for o in range(-BAND, BAND + 1) if o)
CHAINS = 2
CHUNKS = 4
F32 = jnp.float32
BF16 = jnp.bfloat16


def dot(a, b, dims):
    return lax.dot_general(a, b, (dims, ((), ())), preferred_element_type=F32)


def kernel(
    n_row, n_col, scale,
    features, weight, bias, grad_out, tiles, count, dst, src,
    act_out, gf_out, gw_out, gb_out,
    tiles_v, sums, feat_w, wt_v, bias_v, go_v, dst_v, src_v, idx_v, idx_s,
    adj, adj_t, acc, part, part_in, agg_v, dpre_v, act_v, grads, back, back_in, gf_v,
    pay, pay_in, bf_out, bf_in, gw_v, gb_v,
    tile_sem, in_sem, idx_sem, out_sem,
    halo_s, halo_r, part_s, part_r, ga_s, ga_r, bk_s, bk_r, pay_s, pay_r, bf_s, bf_r, ag_s, ag_r,
):
    row = lax.axis_index("row")
    col = lax.axis_index("col")
    node_dev, width = features.shape
    maxt, tile = tiles.shape[1], tiles.shape[2]
    window_tiles = (2 * BAND + 1) * (node_dev // tile)
    dst_tiles = n_col * node_dev // tile
    half = maxt // CHAINS
    group = half // CHUNKS
    steps = bf_out.shape[0]
    w_rows = width // n_col

    def at_row(offset):
        return {"row": lax.rem(row + offset + n_row, n_row)}

    def flip(step):
        bit = 1 << step
        up = lax.rem(row // bit, 2)
        return {"row": row + bit - 2 * bit * up}

    def clamp(index):
        return jnp.minimum(jnp.maximum(index, 0), half)

    def at_col(offset):
        return {"col": lax.rem(col + offset, n_col)}

    barrier = pltpu.get_barrier_semaphore()
    partners = (
        [at_row(o) for o in OFFSETS]
        + [flip(s) for s in range(steps)]
        + [at_col(o) for o in range(1, n_col)]
    )
    for partner in partners:
        pl.semaphore_signal(barrier, inc=1, device_id=partner, device_id_type=MESH)

    small = [
        pltpu.make_async_copy(a, b, in_sem.at[n])
        for n, (a, b) in enumerate(
            [
                (dst, dst_v),
                (src, src_v),
                (features, feat_w.at[pl.ds(BAND * node_dev, node_dev)]),
                (weight, wt_v),
                (bias, bias_v),
                (grad_out, go_v),
            ]
        )
    ]
    for copy in small[:2]:
        copy.start()
    loads = []
    for g in range(CHUNKS):
        for h in range(CHAINS):
            at = pl.ds(h * half + g * group, group)
            copy = pltpu.make_async_copy(tiles.at[0, at], tiles_v.at[at], tile_sem.at[g * CHAINS + h])
            copy.start()
            loads.append(copy)
    for copy in small[2:]:
        copy.start()

    small[0].wait()
    small[1].wait()
    lane = lax.broadcasted_iota(jnp.int32, (1, maxt), 1)
    key = jnp.where(lane < count[0], dst_v[...] * window_tiles + src_v[...], -1).astype(F32)
    key = jnp.broadcast_to(key, (maxt, maxt))
    key_t = key.T
    ri = lax.broadcasted_iota(jnp.int32, (maxt, maxt), 0)
    ci = lax.broadcasted_iota(jnp.int32, (maxt, maxt), 1)
    ri_f = ri.astype(F32)
    prev = jnp.zeros((maxt, maxt), F32)
    for h in range(CHAINS):
        inside = (ri >= h * half) & (ri < ci) & (ci < (h + 1) * half)
        prev = jnp.where((key == key_t) & inside, ri_f + (1.0 - h * half), prev)
    idx_v[0:1, 0:maxt] = jnp.max(prev, 0, keepdims=True).astype(jnp.int32)
    pairs = idx_v.shape[1]
    key_c = jnp.broadcast_to(key_t[:, 0:1], (maxt, pairs))
    pc = lax.broadcasted_iota(jnp.int32, (maxt, pairs), 1).astype(F32)
    pr = lax.broadcasted_iota(jnp.int32, (maxt, pairs), 0)
    for h in range(CHAINS):
        inside = (pr >= h * half) & (pr < (h + 1) * half)
        last = jnp.where((key_c == pc) & inside, pr.astype(F32) + (1.0 - h * half), 0.0)
        idx_v[h + 1 : h + 2, :] = jnp.max(last, 0, keepdims=True).astype(jnp.int32)
    to_scalar = pltpu.make_async_copy(idx_v, idx_s, idx_sem)
    to_scalar.start()

    pl.semaphore_wait(barrier, len(partners))
    halos = []
    for n, o in enumerate(OFFSETS):
        copy = pltpu.make_async_remote_copy(
            src_ref=features,
            dst_ref=feat_w.at[pl.ds((o + BAND) * node_dev, node_dev)],
            send_sem=halo_s.at[n],
            recv_sem=halo_r.at[n],
            device_id=at_row(-o),
            device_id_type=MESH,
        )
        copy.start()
        halos.append(copy)

    for h in range(CHAINS):
        sums[h, 0] = jnp.zeros((tile, tile), F32)
    to_scalar.wait()
    for g in range(CHUNKS):
        for h in range(CHAINS):
            loads[g * CHAINS + h].wait()

        def add(i, carry):
            slot = g * group + i
            for h in range(CHAINS):
                before = clamp(idx_s[0, h * half + slot])
                sums[h, slot + 1] = tiles_v[h * half + slot].astype(F32) + sums[h, before]
            return carry

        lax.fori_loop(0, group, add, 0, unroll=2)

    def place(j, carry):
        cols = pl.ds(pl.multiple_of(j * tile, tile), tile)
        for d in range(dst_tiles):
            total = sums[0, clamp(idx_s[1, d * window_tiles + j])]
            for h in range(1, CHAINS):
                total = total + sums[h, clamp(idx_s[h + 1, d * window_tiles + j])]
            adj[pl.ds(d * tile, tile), cols] = total.astype(BF16)
            adj_t[cols, pl.ds(d * tile, tile)] = total.T.astype(BF16)
        return carry

    lax.fori_loop(0, window_tiles, place, 0)

    for copy in small[2:]:
        copy.wait()

    def window_part(o):
        at = pl.ds((o + BAND) * node_dev, node_dev)
        return dot(adj[:, at], feat_w[at, :], ((1,), (0,)))

    acc[...] = window_part(0)
    for n, o in sorted(enumerate(OFFSETS), key=lambda p: abs(p[1])):
        halos[n].wait_recv()
        acc[...] += window_part(o)
    part[...] = acc[...].astype(BF16)

    mine = pl.ds(pl.multiple_of(col * node_dev, node_dev), node_dev)
    sends = []
    for o in range(1, n_col):
        q = lax.rem(col + o, n_col)
        copy = pltpu.make_async_remote_copy(
            src_ref=part.at[pl.ds(pl.multiple_of(q * node_dev, node_dev), node_dev)],
            dst_ref=part_in.at[col],
            send_sem=part_s.at[o - 1],
            recv_sem=part_r.at[o - 1],
            device_id=at_col(o),
            device_id_type=MESH,
        )
        copy.start()
        sends.append(copy)
    part_in[col] = part[mine, :]
    for copy in sends:
        copy.wait_recv()
    summed = part_in[0].astype(F32)
    for q in range(1, n_col):
        summed = summed + part_in[q].astype(F32)
    agg_v[...] = summed.astype(BF16)

    pre = dot(agg_v[...], wt_v[...], ((1,), (0,))) + bias_v[...]
    sig = jax.nn.sigmoid(pre)
    act_v[...] = (pre * sig).astype(BF16)
    dpre_v[...] = (go_v[...].astype(F32) * sig * (1.0 + pre * (1.0 - sig))).astype(BF16)
    grads[mine, :] = dot(dpre_v[...], wt_v[...], ((1,), (1,))).astype(BF16)
    gathers = []
    for o in range(1, n_col):
        copy = pltpu.make_async_remote_copy(
            src_ref=grads.at[mine],
            dst_ref=grads.at[mine],
            send_sem=ga_s.at[o - 1],
            recv_sem=ga_r.at[o - 1],
            device_id=at_col(o),
            device_id_type=MESH,
        )
        copy.start()
        gathers.append(copy)
    act_copy = pltpu.make_async_copy(act_v, act_out, out_sem.at[0])
    act_copy.start()

    w_term = dot(agg_v[...], dpre_v[...], ((0,), (0,))).astype(BF16)
    b_term = jnp.sum(dpre_v[...].astype(F32), 0, keepdims=True).astype(BF16)
    b_rows = pay.shape[1] - w_rows
    for q in range(n_col):
        pay[q, 0:w_rows, :] = w_term[q * w_rows : (q + 1) * w_rows, :]
        pay[q, w_rows:, :] = jnp.broadcast_to(b_term, (b_rows, b_term.shape[1]))
    pays = []
    for o in range(1, n_col):
        copy = pltpu.make_async_remote_copy(
            src_ref=pay.at[lax.rem(col + o, n_col)],
            dst_ref=pay_in.at[col],
            send_sem=pay_s.at[o - 1],
            recv_sem=pay_r.at[o - 1],
            device_id=at_col(o),
            device_id_type=MESH,
        )
        copy.start()
        pays.append(copy)
    pay_in[col] = pay[col]

    for copy in gathers:
        copy.wait_recv()

    def back_part(o):
        return dot(adj_t[pl.ds((o + BAND) * node_dev, node_dev), :], grads[...], ((1,), (0,)))

    backs = []
    for n, o in enumerate(OFFSETS):
        back[n] = back_part(o).astype(BF16)
        copy = pltpu.make_async_remote_copy(
            src_ref=back.at[n],
            dst_ref=back_in.at[n],
            send_sem=bk_s.at[n],
            recv_sem=bk_r.at[n],
            device_id=at_row(o),
            device_id_type=MESH,
        )
        copy.start()
        backs.append(copy)

    for copy in pays:
        copy.wait_recv()
    value = pay_in[0].astype(F32)
    for q in range(1, n_col):
        value = value + pay_in[q].astype(F32)
    flips = []
    for s in range(steps):
        bf_out[s] = value.astype(BF16)
        copy = pltpu.make_async_remote_copy(
            src_ref=bf_out.at[s],
            dst_ref=bf_in.at[s],
            send_sem=bf_s.at[s],
            recv_sem=bf_r.at[s],
            device_id=flip(s),
            device_id_type=MESH,
        )
        copy.start()
        flips.append(copy)
        if s == 0:
            acc[0:node_dev, :] = back_part(0)
        copy.wait_recv()
        value = bf_out[s].astype(F32) + bf_in[s].astype(F32)
    value = value * (1.0 / scale)
    w_mine = pl.ds(pl.multiple_of(col * w_rows, w_rows), w_rows)
    gw_v[w_mine, :] = value[0:w_rows, :]
    ends = []
    for o in range(1, n_col):
        copy = pltpu.make_async_remote_copy(
            src_ref=gw_v.at[w_mine],
            dst_ref=gw_v.at[w_mine],
            send_sem=ag_s.at[o - 1],
            recv_sem=ag_r.at[o - 1],
            device_id=at_col(o),
            device_id_type=MESH,
        )
        copy.start()
        ends.append(copy)
    gb_v[...] = value[w_rows : w_rows + 1, :]
    gb_copy = pltpu.make_async_copy(gb_v, gb_out, out_sem.at[3])
    gb_copy.start()

    for copy in backs:
        copy.wait_recv()
    total = acc[0:node_dev, :]
    for n in range(len(OFFSETS)):
        total = total + back_in[n].astype(F32)
    gf_v[...] = total.astype(BF16)
    gf_copy = pltpu.make_async_copy(gf_v, gf_out, out_sem.at[1])
    gf_copy.start()
    for copy in ends:
        copy.wait_recv()
    gw_copy = pltpu.make_async_copy(gw_v, gw_out, out_sem.at[2])
    gw_copy.start()
    for copy in halos + sends + gathers + pays + backs + flips + ends:
        copy.wait_send()
    for copy in (act_copy, gf_copy, gb_copy, gw_copy):
        copy.wait()


def local(n_row, n_col, features, weight, bias, grad_out, tiles, tile_count, tile_dst, tile_src):
    node_dev, width = features.shape
    hidden = weight.shape[1]
    maxt, tile = tiles.shape[1], tiles.shape[2]
    window = (2 * BAND + 1) * node_dev
    nodes = n_col * node_dev
    pairs = (nodes // tile) * (window // tile)
    pairs = max(-(-pairs // 128) * 128, maxt)
    steps = n_row.bit_length() - 1
    pay_rows = width // n_col + 16
    offs = len(OFFSETS)
    dma = pltpu.SemaphoreType.DMA
    any_spec = pl.BlockSpec(memory_space=pl.ANY)
    out = pl.pallas_call(
        functools.partial(kernel, n_row, n_col, math.sqrt(node_dev * n_row * n_col)),
        out_shape=(
            jax.ShapeDtypeStruct((node_dev, hidden), BF16),
            jax.ShapeDtypeStruct((node_dev, width), BF16),
            jax.ShapeDtypeStruct((width, hidden), F32),
            jax.ShapeDtypeStruct((1, hidden), F32),
        ),
        in_specs=[any_spec] * 5 + [pl.BlockSpec(memory_space=pltpu.SMEM)] + [any_spec] * 2,
        out_specs=(any_spec,) * 4,
        scratch_shapes=[
            pltpu.VMEM((maxt, tile, tile), BF16),
            pltpu.VMEM((CHAINS, maxt // CHAINS + 1, tile, tile), F32),
            pltpu.VMEM((window, width), BF16),
            pltpu.VMEM((width, hidden), BF16),
            pltpu.VMEM((1, hidden), F32),
            pltpu.VMEM((node_dev, hidden), BF16),
            pltpu.VMEM((1, maxt), jnp.int32),
            pltpu.VMEM((1, maxt), jnp.int32),
            pltpu.VMEM((8, pairs), jnp.int32),
            pltpu.SMEM((8, pairs), jnp.int32),
            pltpu.VMEM((nodes, window), BF16),
            pltpu.VMEM((window, nodes), BF16),
            pltpu.VMEM((nodes, width), F32),
            pltpu.VMEM((nodes, width), BF16),
            pltpu.VMEM((n_col, node_dev, width), BF16),
            pltpu.VMEM((node_dev, width), BF16),
            pltpu.VMEM((node_dev, hidden), BF16),
            pltpu.VMEM((node_dev, hidden), BF16),
            pltpu.VMEM((nodes, width), BF16),
            pltpu.VMEM((offs, node_dev, width), BF16),
            pltpu.VMEM((offs, node_dev, width), BF16),
            pltpu.VMEM((node_dev, width), BF16),
            pltpu.VMEM((n_col, pay_rows, hidden), BF16),
            pltpu.VMEM((n_col, pay_rows, hidden), BF16),
            pltpu.VMEM((steps, pay_rows, hidden), BF16),
            pltpu.VMEM((steps, pay_rows, hidden), BF16),
            pltpu.VMEM((width, hidden), F32),
            pltpu.VMEM((1, hidden), F32),
            dma((CHAINS * CHUNKS,)),
            dma((6,)),
            dma(()),
            dma((4,)),
        ]
        + [
            dma((n,))
            for n in (offs, n_col - 1, n_col - 1, offs, n_col - 1, steps, n_col - 1)
            for _ in range(2)
        ],
        compiler_params=pltpu.CompilerParams(
            collective_id=0, has_side_effects=True, vmem_limit_bytes=60 * 1024 * 1024
        ),
        name="graph_conv",
    )(features, weight, bias.reshape(1, hidden), grad_out, tiles, tile_count, tile_dst, tile_src)
    return out[0], out[1], out[2], out[3].reshape(hidden)


def solution(mesh):
    in_specs = (
        P(("row", "col"), None),
        P(),
        P(),
        P(("row", "col"), None),
        P(("row", "col"), None, None, None),
        P(("row", "col")),
        P(("row", "col"), None),
        P(("row", "col"), None),
    )
    out_specs = (P(("row", "col"), None), P(("row", "col"), None), P(), P())
    body = functools.partial(local, mesh.shape["row"], mesh.shape["col"])
    return jax.shard_map(body, mesh=mesh, in_specs=in_specs, out_specs=out_specs, check_vma=False)
```

time: 248 us -> 39.1 us (0.16)
  waiting for transfers between devices: 109 us -> 0 us
  blocking collectives: 42.3 us -> 0 us
  starting transfers between devices: 37.9 us -> 0 us
  Pallas kernels: 0 us -> 31.3 us
  other arithmetic: 19.5 us -> 0 us
  between operations: 14.9 us -> 1.29 us
  matrix products: 11.7 us -> 0 us
  local copies, waits for them, and re-layouts: 11.3 us -> 5.85 us
    psum x1 -> x0, waiting for transfers between devices: 80 us -> none  [local(): lax.psum((weight_term, bias_term), ('row', 'col'))]
    psum x1 -> x0, blocking collectives: 40.4 us -> none  [local(): lax.psum((weight_term, bias_term), ('row', 'col'))]
    ppermute x8 -> x0, starting transfers between devices: 37.8 us -> none  [shifted(): return lax.ppermute(value, axis, pairs)]
    pallas_call x0 -> x1, Pallas kernels: none -> 31.3 us  [local(): pl.pallas_call(functools.partial(kernel, n_row, n_col, math.sqrt(node_dev...]
    reduce_scatter x1 -> x0, waiting for transfers between devices: 23.7 us -> none  [local(): lax.psum_scatter(acc.reshape(dst_tiles * tile, in_width).astype(jnp.bfloa...]
    dot_general x9 -> x0, matrix products: 11.7 us -> none  [the longest x3 4.01 us: back_step(): jnp.einsum('kji,kjh->kih', tile_block, block_grads[dst_block], preferred_...]
    scatter-add x6 -> x0, other arithmetic: 9.61 us -> none  [the longest x3 4.81 us: back_step(): return acc_back.at[src_block].add(contrib * live[:, None, None])]
    ppermute x8 -> x0, waiting for transfers between devices: 5.53 us -> none  [shifted(): return lax.ppermute(value, axis, pairs)]
  transfers between devices with their start and end apart: 10 -> 0, of which waited for: 3 -> 0; matrix products, arithmetic and copies ran while one was open for 9% -> 0% of each run, Pallas kernels for 0% -> 0%
where the time goes in v1:
time: 39.1 us; the launch traced here: 38.4 us
  Pallas kernels  31.3 us (80%)
  local copies, waits for them, and re-layouts  5.85 us (15%)
  between operations  1.29 us (3%)
    pallas_call x1, Pallas kernels, local(): pl.pallas_call(functools.partial(kernel, n_row, n_col, math.sqrt(node_dev...  31.3 us
    unnamed x4, local copies, waits for them, and re-layouts  5.85 us

profile of v1, /device:TPU:0, one launch (start us, length us, event | category | flops | bytes accessed | tf_op | source)
XLA Modules:
  0.0 38.4 jit_solution(12530738642360020053)
XLA Ops:
  1.3 31.3 %graph_conv.1 = (bf16[256,256]{1,0:T(8,128)(2,1)}, bf16[256,128]{1,0:T(8,128)(2,1)}, f32[128,256]{1,0:T(8,128)}, f32[1,256]{1,0:T(1,128)}) custom-call(bf16[256,128]{1,0:T(8,128)(2,1)} %features.1, bf16[128,256]{1,0:T(8,128)(2,1)} %weight.1, f32[1,256]{1,0:T(1,128)} %bitcast.2, bf16[256,256]{1,0:T(8,128)(2,1)} %grad_out.1, bf16[1,128,128,128]{3,2,1,0:T(8,128)(2,1)} %tiles.1, ...), custom_call_target="tpu_custom_call" | custom-call | tf_op jit(solution)/shard_map/graph_conv/pallas_call | solution.py:327
  32.6 1.6 %copy.17 = bf16[256,256]{1,0:T(8,128)(2,1)} copy(bf16[256,256]{1,0:T(8,128)(2,1)} %get-tuple-element.16) | data formatting | bytes 262144
  34.1 1.5 %copy.18 = bf16[256,128]{1,0:T(8,128)(2,1)} copy(bf16[256,128]{1,0:T(8,128)(2,1)} %get-tuple-element.17) | data formatting | bytes 131072
  35.6 1.6 %copy.19 = f32[128,256]{1,0:T(8,128)} copy(f32[128,256]{1,0:T(8,128)} %get-tuple-element.18) | data formatting | bytes 262144
  37.2 1.2 %copy.20 = f32[256]{0:T(256)} copy(f32[256]{0:T(256)} %bitcast.3) | data formatting | bytes 2048

commit v2 on v1

--- a/solution.py
+++ b/solution.py
@@ -196,22 +196,6 @@
     sig = jax.nn.sigmoid(pre)
     act_v[...] = (pre * sig).astype(BF16)
     dpre_v[...] = (go_v[...].astype(F32) * sig * (1.0 + pre * (1.0 - sig))).astype(BF16)
-    grads[mine, :] = dot(dpre_v[...], wt_v[...], ((1,), (1,))).astype(BF16)
-    gathers = []
-    for o in range(1, n_col):
-        copy = pltpu.make_async_remote_copy(
-            src_ref=grads.at[mine],
-            dst_ref=grads.at[mine],
-            send_sem=ga_s.at[o - 1],
-            recv_sem=ga_r.at[o - 1],
-            device_id=at_col(o),
-            device_id_type=MESH,
-        )
-        copy.start()
-        gathers.append(copy)
-    act_copy = pltpu.make_async_copy(act_v, act_out, out_sem.at[0])
-    act_copy.start()
-
     w_term = dot(agg_v[...], dpre_v[...], ((0,), (0,))).astype(BF16)
     b_term = jnp.sum(dpre_v[...].astype(F32), 0, keepdims=True).astype(BF16)
     b_rows = pay.shape[1] - w_rows
@@ -232,6 +216,22 @@
         pays.append(copy)
     pay_in[col] = pay[col]
 
+    grads[mine, :] = dot(dpre_v[...], wt_v[...], ((1,), (1,))).astype(BF16)
+    gathers = []
+    for o in range(1, n_col):
+        copy = pltpu.make_async_remote_copy(
+            src_ref=grads.at[mine],
+            dst_ref=grads.at[mine],
+            send_sem=ga_s.at[o - 1],
+            recv_sem=ga_r.at[o - 1],
+            device_id=at_col(o),
+            device_id_type=MESH,
+        )
+        copy.start()
+        gathers.append(copy)
+    act_copy = pltpu.make_async_copy(act_v, act_out, out_sem.at[0])
+    act_copy.start()
+
     for copy in gathers:
         copy.wait_recv()
 
@@ -309,6 +309,13 @@
         copy.wait_send()
     for copy in (act_copy, gf_copy, gb_copy, gw_copy):
         copy.wait()
+
+
+def finish(act_in, gf_in, gw_in, gb_in, act_out, gf_out, gw_out, gb_out):
+    act_out[...] = act_in[...]
+    gf_out[...] = gf_in[...]
+    gw_out[...] = gw_in[...]
+    gb_out[...] = gb_in[...]
 
 
 def local(n_row, n_col, features, weight, bias, grad_out, tiles, tile_count, tile_dst, tile_src):
@@ -378,6 +385,14 @@
         ),
         name="graph_conv",
     )(features, weight, bias.reshape(1, hidden), grad_out, tiles, tile_count, tile_dst, tile_src)
+    vmem = pl.BlockSpec(memory_space=pltpu.VMEM)
+    out = pl.pallas_call(
+        finish,
+        out_shape=tuple(jax.ShapeDtypeStruct(o.shape, o.dtype) for o in out),
+        in_specs=[vmem] * 4,
+        out_specs=(vmem,) * 4,
+        name="finish",
+    )(*out)
     return out[0], out[1], out[2], out[3].reshape(hidden)
 
 

time: 39.1 us -> 35 us (0.90)
  local copies, waits for them, and re-layouts: 5.85 us -> 0 us
  Pallas kernels: 31.3 us -> 33.1 us
    unnamed x4 -> x0, local copies, waits for them, and re-layouts: 5.85 us -> none
    pallas_call x0 -> x1, Pallas kernels: none -> 1.74 us  [local(): pl.pallas_call(finish, out_shape=tuple((jax.ShapeDtypeStruct(o.shape, o.d...]
where the time goes in v2:
time: 35 us; the launch traced here: 34.3 us
  Pallas kernels  33.1 us (95%)
  between operations  1.29 us (4%)
    pallas_call x1, Pallas kernels, local(): pl.pallas_call(functools.partial(kernel, n_row, n_col, math.sqrt(node_dev...  31.3 us
    pallas_call x1, Pallas kernels, local(): pl.pallas_call(finish, out_shape=tuple((jax.ShapeDtypeStruct(o.shape, o.d...  1.74 us

profile of v2, /device:TPU:0, one launch (start us, length us, event | category | flops | bytes accessed | tf_op | source)
XLA Modules:
  0.0 34.3 jit_solution(1221340315206344808)
XLA Ops:
  1.3 31.3 %graph_conv.1 = (bf16[256,256]{1,0:T(8,128)(2,1)}, bf16[256,128]{1,0:T(8,128)(2,1)}, f32[128,256]{1,0:T(8,128)}, f32[1,256]{1,0:T(1,128)}) custom-call(bf16[256,128]{1,0:T(8,128)(2,1)} %features.1, bf16[128,256]{1,0:T(8,128)(2,1)} %weight.1, f32[1,256]{1,0:T(1,128)} %bitcast.2, bf16[256,256]{1,0:T(8,128)(2,1)} %grad_out.1, bf16[1,128,128,128]{3,2,1,0:T(8,128)(2,1)} %tiles.1, ...), custom_call_target="tpu_custom_call" | custom-call | tf_op jit(solution)/shard_map/graph_conv/pallas_call | solution.py:334
  32.6 1.7 %finish.1 = (bf16[256,256]{1,0:T(8,128)(2,1)}, bf16[256,128]{1,0:T(8,128)(2,1)}, f32[128,256]{1,0:T(8,128)}, f32[1,256]{1,0:T(1,128)}) custom-call(bf16[256,256]{1,0:T(8,128)(2,1)} %get-tuple-element.12.act_in, bf16[256,128]{1,0:T(8,128)(2,1)} %get-tuple-element.13.gf_in, f32[128,256]{1,0:T(8,128)} %get-tuple-element.14.gw_in, f32[1,256]{1,0:T(1,128)} %get-tuple-element.15.gb_in), custom_call_target="tpu_custom_call" | custom-call | tf_op jit(solution)/shard_map/finish/pallas_call | solution.py:389

commit v3 on v2

--- a/solution.py
+++ b/solution.py
@@ -22,12 +22,12 @@
 
 
 def kernel(
-    n_row, n_col, scale,
+    n_row, n_col,
     features, weight, bias, grad_out, tiles, count, dst, src,
     act_out, gf_out, gw_out, gb_out,
     tiles_v, sums, feat_w, wt_v, bias_v, go_v, dst_v, src_v, idx_v, idx_s,
     adj, adj_t, acc, part, part_in, agg_v, dpre_v, act_v, grads, back, back_in, gf_v,
-    pay, pay_in, bf_out, bf_in, gw_v, gb_v,
+    pay, pay_in, bf_in, gw_v, gb_v,
     tile_sem, in_sem, idx_sem, out_sem,
     halo_s, halo_r, part_s, part_r, ga_s, ga_r, bk_s, bk_r, pay_s, pay_r, bf_s, bf_r, ag_s, ag_r,
 ):
@@ -39,16 +39,24 @@
     dst_tiles = n_col * node_dev // tile
     half = maxt // CHAINS
     group = half // CHUNKS
-    steps = bf_out.shape[0]
-    w_rows = width // n_col
+    n_plane, pay_rows = pay.shape[0], pay.shape[1]
+    low_n = n_plane // n_col
+    high_n = n_row // low_n
+    w_rows = width // n_plane
+    b_at = gw_out.shape[1]
 
     def at_row(offset):
         return {"row": lax.rem(row + offset + n_row, n_row)}
 
-    def flip(step):
-        bit = 1 << step
-        up = lax.rem(row // bit, 2)
-        return {"row": row + bit - 2 * bit * up}
+    low, high = lax.rem(row, low_n), row // low_n
+    place_id = low * n_col + col
+
+    def in_plane(offset):
+        q = lax.rem(place_id + offset, n_plane)
+        return q, {"row": high * low_n + q // n_col, "col": lax.rem(q, n_col)}
+
+    def across(offset):
+        return {"row": lax.rem(high + offset, high_n) * low_n + low}
 
     def clamp(index):
         return jnp.minimum(jnp.maximum(index, 0), half)
@@ -59,8 +67,8 @@
     barrier = pltpu.get_barrier_semaphore()
     partners = (
         [at_row(o) for o in OFFSETS]
-        + [flip(s) for s in range(steps)]
-        + [at_col(o) for o in range(1, n_col)]
+        + [in_plane(o)[1] for o in range(1, n_plane)]
+        + [across(o) for o in range(1, high_n)]
     )
     for partner in partners:
         pl.semaphore_signal(barrier, inc=1, device_id=partner, device_id_type=MESH)
@@ -198,23 +206,23 @@
     dpre_v[...] = (go_v[...].astype(F32) * sig * (1.0 + pre * (1.0 - sig))).astype(BF16)
     w_term = dot(agg_v[...], dpre_v[...], ((0,), (0,))).astype(BF16)
     b_term = jnp.sum(dpre_v[...].astype(F32), 0, keepdims=True).astype(BF16)
-    b_rows = pay.shape[1] - w_rows
-    for q in range(n_col):
+    for q in range(n_plane):
         pay[q, 0:w_rows, :] = w_term[q * w_rows : (q + 1) * w_rows, :]
-        pay[q, w_rows:, :] = jnp.broadcast_to(b_term, (b_rows, b_term.shape[1]))
+        pay[q, b_at:, :] = jnp.broadcast_to(b_term, (pay_rows - b_at, b_term.shape[1]))
     pays = []
-    for o in range(1, n_col):
-        copy = pltpu.make_async_remote_copy(
-            src_ref=pay.at[lax.rem(col + o, n_col)],
-            dst_ref=pay_in.at[col],
+    for o in range(1, n_plane):
+        q, target = in_plane(o)
+        copy = pltpu.make_async_remote_copy(
+            src_ref=pay.at[q],
+            dst_ref=pay_in.at[place_id],
             send_sem=pay_s.at[o - 1],
             recv_sem=pay_r.at[o - 1],
-            device_id=at_col(o),
+            device_id=target,
             device_id_type=MESH,
         )
         copy.start()
         pays.append(copy)
-    pay_in[col] = pay[col]
+    pay_in[place_id] = pay[place_id]
 
     grads[mine, :] = dot(dpre_v[...], wt_v[...], ((1,), (1,))).astype(BF16)
     gathers = []
@@ -255,41 +263,41 @@
     for copy in pays:
         copy.wait_recv()
     value = pay_in[0].astype(F32)
-    for q in range(1, n_col):
+    for q in range(1, n_plane):
         value = value + pay_in[q].astype(F32)
+    bf_in[high] = value.astype(BF16)
     flips = []
-    for s in range(steps):
-        bf_out[s] = value.astype(BF16)
-        copy = pltpu.make_async_remote_copy(
-            src_ref=bf_out.at[s],
-            dst_ref=bf_in.at[s],
-            send_sem=bf_s.at[s],
-            recv_sem=bf_r.at[s],
-            device_id=flip(s),
+    for o in range(1, high_n):
+        copy = pltpu.make_async_remote_copy(
+            src_ref=bf_in.at[high],
+            dst_ref=bf_in.at[high],
+            send_sem=bf_s.at[o - 1],
+            recv_sem=bf_r.at[o - 1],
+            device_id=across(o),
             device_id_type=MESH,
         )
         copy.start()
         flips.append(copy)
-        if s == 0:
-            acc[0:node_dev, :] = back_part(0)
-        copy.wait_recv()
-        value = bf_out[s].astype(F32) + bf_in[s].astype(F32)
-    value = value * (1.0 / scale)
-    w_mine = pl.ds(pl.multiple_of(col * w_rows, w_rows), w_rows)
-    gw_v[w_mine, :] = value[0:w_rows, :]
+    acc[0:node_dev, :] = back_part(0)
+    for copy in flips:
+        copy.wait_recv()
+    value = bf_in[0].astype(F32)
+    for q in range(1, high_n):
+        value = value + bf_in[q].astype(F32)
+    gw_v[place_id] = value[0:b_at, :].astype(BF16)
     ends = []
-    for o in range(1, n_col):
-        copy = pltpu.make_async_remote_copy(
-            src_ref=gw_v.at[w_mine],
-            dst_ref=gw_v.at[w_mine],
+    for o in range(1, n_plane):
+        copy = pltpu.make_async_remote_copy(
+            src_ref=gw_v.at[place_id],
+            dst_ref=gw_v.at[place_id],
             send_sem=ag_s.at[o - 1],
             recv_sem=ag_r.at[o - 1],
-            device_id=at_col(o),
+            device_id=in_plane(o)[1],
             device_id_type=MESH,
         )
         copy.start()
         ends.append(copy)
-    gb_v[...] = value[w_rows : w_rows + 1, :]
+    gb_v[...] = value[b_at : b_at + 1, :]
     gb_copy = pltpu.make_async_copy(gb_v, gb_out, out_sem.at[3])
     gb_copy.start()
 
@@ -311,11 +319,13 @@
         copy.wait()
 
 
-def finish(act_in, gf_in, gw_in, gb_in, act_out, gf_out, gw_out, gb_out):
+def finish(scale, act_in, gf_in, gw_in, gb_in, act_out, gf_out, gw_out, gb_out):
     act_out[...] = act_in[...]
     gf_out[...] = gf_in[...]
-    gw_out[...] = gw_in[...]
-    gb_out[...] = gb_in[...]
+    rows = gw_out.shape[0] // gw_in.shape[0]
+    for q in range(gw_in.shape[0]):
+        gw_out[q * rows : (q + 1) * rows, :] = gw_in[q, 0:rows, :].astype(F32) * (1.0 / scale)
+    gb_out[...] = gb_in[...] * (1.0 / scale)
 
 
 def local(n_row, n_col, features, weight, bias, grad_out, tiles, tile_count, tile_dst, tile_src):
@@ -326,17 +336,22 @@
     nodes = n_col * node_dev
     pairs = (nodes // tile) * (window // tile)
     pairs = max(-(-pairs // 128) * 128, maxt)
-    steps = n_row.bit_length() - 1
-    pay_rows = width // n_col + 16
+    low_n = math.isqrt(n_row)
+    while n_row % low_n:
+        low_n -= 1
+    high_n = n_row // low_n
+    n_plane = low_n * n_col
+    b_at = -(-(width // n_plane) // 8) * 8
+    pay_rows = b_at + 8
     offs = len(OFFSETS)
     dma = pltpu.SemaphoreType.DMA
     any_spec = pl.BlockSpec(memory_space=pl.ANY)
     out = pl.pallas_call(
-        functools.partial(kernel, n_row, n_col, math.sqrt(node_dev * n_row * n_col)),
+        functools.partial(kernel, n_row, n_col),
         out_shape=(
             jax.ShapeDtypeStruct((node_dev, hidden), BF16),
             jax.ShapeDtypeStruct((node_dev, width), BF16),
-            jax.ShapeDtypeStruct((width, hidden), F32),
+            jax.ShapeDtypeStruct((n_plane, b_at, hidden), BF16),
             jax.ShapeDtypeStruct((1, hidden), F32),
         ),
         in_specs=[any_spec] * 5 + [pl.BlockSpec(memory_space=pltpu.SMEM)] + [any_spec] * 2,
@@ -364,11 +379,10 @@
             pltpu.VMEM((offs, node_dev, width), BF16),
             pltpu.VMEM((offs, node_dev, width), BF16),
             pltpu.VMEM((node_dev, width), BF16),
-            pltpu.VMEM((n_col, pay_rows, hidden), BF16),
-            pltpu.VMEM((n_col, pay_rows, hidden), BF16),
-            pltpu.VMEM((steps, pay_rows, hidden), BF16),
-            pltpu.VMEM((steps, pay_rows, hidden), BF16),
-            pltpu.VMEM((width, hidden), F32),
+            pltpu.VMEM((n_plane, pay_rows, hidden), BF16),
+            pltpu.VMEM((n_plane, pay_rows, hidden), BF16),
+            pltpu.VMEM((high_n, pay_rows, hidden), BF16),
+            pltpu.VMEM((n_plane, b_at, hidden), BF16),
             pltpu.VMEM((1, hidden), F32),
             dma((CHAINS * CHUNKS,)),
             dma((6,)),
@@ -377,7 +391,7 @@
         ]
         + [
             dma((n,))
-            for n in (offs, n_col - 1, n_col - 1, offs, n_col - 1, steps, n_col - 1)
+            for n in (offs, n_col - 1, n_col - 1, offs, n_plane - 1, high_n - 1, n_plane - 1)
             for _ in range(2)
         ],
         compiler_params=pltpu.CompilerParams(
@@ -387,8 +401,13 @@
     )(features, weight, bias.reshape(1, hidden), grad_out, tiles, tile_count, tile_dst, tile_src)
     vmem = pl.BlockSpec(memory_space=pltpu.VMEM)
     out = pl.pallas_call(
-        finish,
-        out_shape=tuple(jax.ShapeDtypeStruct(o.shape, o.dtype) for o in out),
+        functools.partial(finish, math.sqrt(node_dev * n_row * n_col)),
+        out_shape=(
+            jax.ShapeDtypeStruct((node_dev, hidden), BF16),
+            jax.ShapeDtypeStruct((node_dev, width), BF16),
+            jax.ShapeDtypeStruct((width, hidden), F32),
+            jax.ShapeDtypeStruct((1, hidden), F32),
+        ),
         in_specs=[vmem] * 4,
         out_specs=(vmem,) * 4,
         name="finish",

time: 35 us -> 29.9 us (0.85); the launches traced: 34.3 us -> 29.8 us
  Pallas kernels: 33.1 us -> 28.5 us
    pallas_call x2, Pallas kernels: 33.1 us -> 28.5 us  [the longest x1 26.8 us: local(): pl.pallas_call(functools.partial(kernel, n_row, n_col), out_shape=(jax.Sh...]
where the time goes in v3:
time: 29.9 us; the launch traced here: 29.8 us
  Pallas kernels  28.5 us (95%)
  between operations  1.29 us (4%)
    pallas_call x1, Pallas kernels, local(): pl.pallas_call(functools.partial(kernel, n_row, n_col), out_shape=(jax.Sh...  26.8 us
    pallas_call x1, Pallas kernels, local(): pl.pallas_call(functools.partial(finish, math.sqrt(node_dev * n_row * n_c...  1.68 us

profile of v3, /device:TPU:0, one launch (start us, length us, event | category | flops | bytes accessed | tf_op | source)
XLA Modules:
  0.0 29.8 jit_solution(1694977123876227797)
XLA Ops:
  1.3 26.8 %graph_conv.1 = (bf16[256,256]{1,0:T(8,128)(2,1)}, bf16[256,128]{1,0:T(8,128)(2,1)}, bf16[8,16,256]{2,1,0:T(8,128)(2,1)}, f32[1,256]{1,0:T(1,128)}) custom-call(bf16[256,128]{1,0:T(8,128)(2,1)} %features.1, bf16[128,256]{1,0:T(8,128)(2,1)} %weight.1, f32[1,256]{1,0:T(1,128)} %bitcast.2, bf16[256,256]{1,0:T(8,128)(2,1)} %grad_out.1, ...), custom_call_target="tpu_custom_call" | custom-call | tf_op jit(solution)/shard_map/graph_conv/pallas_call | solution.py:349
  28.1 1.7 %finish.1 = (bf16[256,256]{1,0:T(8,128)(2,1)}, bf16[256,128]{1,0:T(8,128)(2,1)}, f32[128,256]{1,0:T(8,128)}, f32[1,256]{1,0:T(1,128)}) custom-call(bf16[256,256]{1,0:T(8,128)(2,1)} %get-tuple-element.12.act_in, bf16[256,128]{1,0:T(8,128)(2,1)} %get-tuple-element.13.gf_in, bf16[8,16,256]{2,1,0:T(8,128)(2,1)} %get-tuple-element.14.gw_in, ...), custom_call_target="tpu_custom_call" | custom-call | tf_op jit(solution)/shard_map/finish/pallas_call | solution.py:403

commit v4 on v3

--- a/solution.py
+++ b/solution.py
@@ -247,7 +247,7 @@
         return dot(adj_t[pl.ds((o + BAND) * node_dev, node_dev), :], grads[...], ((1,), (0,)))
 
     backs = []
-    for n, o in enumerate(OFFSETS):
+    for n, o in list(enumerate(OFFSETS))[:2]:
         back[n] = back_part(o).astype(BF16)
         copy = pltpu.make_async_remote_copy(
             src_ref=back.at[n],
@@ -278,6 +278,19 @@
         )
         copy.start()
         flips.append(copy)
+    for n, o in list(enumerate(OFFSETS))[2:]:
+        back[n] = back_part(o).astype(BF16)
+        copy = pltpu.make_async_remote_copy(
+            src_ref=back.at[n],
+            dst_ref=back_in.at[n],
+            send_sem=bk_s.at[n],
+            recv_sem=bk_r.at[n],
+            device_id=at_row(o),
+            device_id_type=MESH,
+        )
+        copy.start()
+        backs.append(copy)
+
     acc[0:node_dev, :] = back_part(0)
     for copy in flips:
         copy.wait_recv()

time: 29.9 us -> 28.8 us (0.963)
  Pallas kernels: 28.5 us -> 27.4 us
    pallas_call x1, Pallas kernels: 26.8 us -> 25.7 us  [local(): pl.pallas_call(functools.partial(kernel, n_row, n_col), out_shape=(jax.Sh...]
where the time goes in v4:
time: 28.8 us; the launch traced here: 28.7 us
  Pallas kernels  27.4 us (95%)
  between operations  1.29 us (4%)
    pallas_call x1, Pallas kernels, local(): pl.pallas_call(functools.partial(kernel, n_row, n_col), out_shape=(jax.Sh...  25.7 us
    pallas_call x1, Pallas kernels, local(): pl.pallas_call(functools.partial(finish, math.sqrt(node_dev * n_row * n_c...  1.68 us

profile of v4, /device:TPU:0, one launch (start us, length us, event | category | flops | bytes accessed | tf_op | source)
XLA Modules:
  0.0 28.7 jit_solution(10896771756430244167)
XLA Ops:
  1.3 25.7 %graph_conv.1 = (bf16[256,256]{1,0:T(8,128)(2,1)}, bf16[256,128]{1,0:T(8,128)(2,1)}, bf16[8,16,256]{2,1,0:T(8,128)(2,1)}, f32[1,256]{1,0:T(1,128)}) custom-call(bf16[256,128]{1,0:T(8,128)(2,1)} %features.1, bf16[128,256]{1,0:T(8,128)(2,1)} %weight.1, f32[1,256]{1,0:T(1,128)} %bitcast.2, bf16[256,256]{1,0:T(8,128)(2,1)} %grad_out.1, ...), custom_call_target="tpu_custom_call" | custom-call | tf_op jit(solution)/shard_map/graph_conv/pallas_call | solution.py:362
  27.0 1.7 %finish.1 = (bf16[256,256]{1,0:T(8,128)(2,1)}, bf16[256,128]{1,0:T(8,128)(2,1)}, f32[128,256]{1,0:T(8,128)}, f32[1,256]{1,0:T(1,128)}) custom-call(bf16[256,256]{1,0:T(8,128)(2,1)} %get-tuple-element.12.act_in, bf16[256,128]{1,0:T(8,128)(2,1)} %get-tuple-element.13.gf_in, bf16[8,16,256]{2,1,0:T(8,128)(2,1)} %get-tuple-element.14.gw_in, ...), custom_call_target="tpu_custom_call" | custom-call | tf_op jit(solution)/shard_map/finish/pallas_call | solution.py:416
